TPU v7x, 32 devices: a whole 2x2x4 slice. The times are simulated.
32 devices in a mesh: wide: 8 (over y, x, core), shard: 4 (over z).
Axes of the slice: x: 2, y: 2, z: 4, core: 2. Of those that a mesh axis runs over, the one named last changes fastest.
Arguments:
- tokens: bfloat16 [32768, 1152], P(('wide', 'shard')), may hold values from -6 to 6
- seg_ids: int32 [32768], P(('wide', 'shard')), may hold values from -1 to 63, as said below
- cotangent: bfloat16 [32768, 1152], P(('wide', 'shard')), may hold values from -6 to 6
- params: float32 [23296, 1152], P('shard'), may hold values from -6 to 6
- gains: float32 [4, 1152], P(None, 'shard'), may hold values from -0.06 to 0.06
- first_moment: float32 [23296, 1152], P('shard'), may hold values from -119.47276 to 119.47276
- second_moment: float32 [23296, 1152], P('shard'), may hold values from 1736.704 to 6881.28
- gain_first: float32 [4, 1152], P(None, 'shard'), may hold values from -119.47276 to 119.47276
- gain_second: float32 [4, 1152], P(None, 'shard'), may hold values from 1736.704 to 6881.28
Outputs:
- result: bfloat16 [32768, 1152], P(('wide', 'shard'))
- input_grad: bfloat16 [32768, 1152], P(('wide', 'shard'))
- row_grad: float32 [23296, 1152], P('shard')
- gain_grad: float32 [4, 1152], P(None, 'shard')
- new_params: float32 [23296, 1152], P('shard')
- new_gains: float32 [4, 1152], P(None, 'shard')
- new_first: float32 [23296, 1152], P('shard')
- new_second: float32 [23296, 1152], P('shard')
- new_gain_first: float32 [4, 1152], P(None, 'shard')
- new_gain_second: float32 [4, 1152], P(None, 'shard')
Inputs may be any that keep to these rules, and one draw needn't show every extreme that they name: `seg_ids`: within each device's 1024 slots the ids start at 0, never fall, and each id covers consecutive slots of one sequence; -1 marks the empty slots at the end of a device; some device holds one sequence of 1024 tokens, some device has empty slots, and some device holds 64 sequences.
All inputs are finite; a program needn't handle non-finite values.
Results may differ from a plain program's by a relative error of at most 0.018.
The roundings to bfloat16 on the way count: a program that leaves them out, or rounds other values in their place, can miss the bound.
Values may be sent and summed in bfloat16 or wider, within the bound.
No kernel may reach another device: no remote copies, remote signals or barrier semaphores. Data moves between devices by JAX's collectives and lax.ppermute only.
A program may use at most 704 MiB of HBM per device.

v0:
```python
import jax
import jax.numpy as jnp
from jax import lax
from jax.experimental import pallas as pl
from jax.experimental.pallas import tpu as pltpu
from jax.sharding import Mesh
from jax.sharding import PartitionSpec as P


D = 1152
FF = 6912
HEADS = 4
KV_HEADS = 1
HD = 256
WINDOW = 512


norm_epsilon = 1e-06
softcap_limit = 50.0
rope_base = 10000.0
beta_first = 0.9
beta_second = 0.95
learn_rate = 0.02
adam_epsilon = 1e-08
weight_decay = 0.1
adam_step = 10.0
masked_floor = -1e30


def rms_scale(values, gain_row):
    return (
        values
        * lax.rsqrt(jnp.mean(values * values, axis=-1, keepdims=True) + norm_epsilon)
        * (1.0 + gain_row)
    )


def positions_of(segments):
    index_row = jnp.arange(segments.shape[0], dtype=jnp.int32)
    previous = jnp.concatenate([segments[:1] - 1, segments[:-1]])
    first_slot = lax.cummax(jnp.where(segments != previous, index_row, 0), axis=0)
    return index_row - first_slot


def rotary_tables(positions, head_width):
    half_width = head_width // 2
    frequency = rope_base ** (-2.0 * jnp.arange(half_width, dtype=jnp.float32) / head_width)
    angles = positions.astype(jnp.float32)[:, None] * frequency[None, :]
    return (jnp.cos(angles), jnp.sin(angles))


def rotate(values, cosine_table, sine_table):
    half_width = values.shape[-1] // 2
    first_half = values[..., :half_width]
    second_half = values[..., half_width:]
    cosine_part = cosine_table[:, None, :]
    sine_part = sine_table[:, None, :]
    return jnp.concatenate(
        [
            first_half * cosine_part - second_half * sine_part,
            second_half * cosine_part + first_half * sine_part,
        ],
        axis=-1,
    )


def contract_rows(left_side, right_side):
    return lax.dot_general(
        left_side, right_side, (((0,), (0,)), ((), ())), preferred_element_type=jnp.float32
    )


def times_transposed(left_side, right_side):
    return lax.dot_general(
        left_side, right_side, (((1,), (1,)), ((), ())), preferred_element_type=jnp.float32
    )


def block_mask(query_segments, key_segments, first_row):
    query_index = first_row + jnp.arange(query_segments.shape[0], dtype=jnp.int32)
    key_index = jnp.arange(key_segments.shape[0], dtype=jnp.int32)
    return (
        (query_segments[:, None] == key_segments[None, :])
        & (key_index[None, :] <= query_index[:, None])
        & (query_index[:, None] - key_index[None, :] < WINDOW)
    )


def adam_update(param_old, grad_sum, first_old, second_old, decay_rate):
    first_new = beta_first * first_old + (1.0 - beta_first) * grad_sum
    second_new = beta_second * second_old + (1.0 - beta_second) * grad_sum * grad_sum
    corrected = (
        first_new
        / (1.0 - beta_first**adam_step)
        / (jnp.sqrt(second_new / (1.0 - beta_second**adam_step)) + adam_epsilon)
    )
    return (param_old - learn_rate * (corrected + decay_rate * param_old), first_new, second_new)


def power_of_two(count):
    return count & (count - 1) == 0


WIDE = ("chip", "core")


def wide_size():
    return lax.axis_size("chip") * lax.axis_size("core")


def butterfly_sum(values, axis_name, count):
    if not power_of_two(count):
        return lax.psum(values, axis_name)
    step = 1
    while step < count:
        values = values + lax.ppermute(values, axis_name, [(i, i ^ step) for i in range(count)])
        step *= 2
    return values


def gather_columns(values, axis_name):
    count = lax.axis_size(axis_name)
    index = lax.axis_index(axis_name)
    width = values.shape[1]
    whole = jnp.zeros((values.shape[0], width * count), values.dtype)
    whole = lax.dynamic_update_slice_in_dim(whole, values, index * width, axis=1)
    for shift in range(1, count):
        moved = lax.ppermute(values, axis_name, [(i, (i + shift) % count) for i in range(count)])
        source = lax.rem(index + count - shift, count)
        whole = lax.dynamic_update_slice_in_dim(whole, moved, source * width, axis=1)
    return whole


def spread_first(rows):
    place = lax.axis_index("shard")
    far = lax.ppermute(rows, "shard", [(0, 2)])
    rows = jnp.where(place == 0, rows, far)
    near = lax.ppermute(rows, "shard", [(0, 1), (2, 3)])
    rows = jnp.where(lax.rem(place, 2) == 1, near, rows)
    index = lax.axis_index(WIDE)
    blocks = {0: rows}
    for bit in (4, 2, 1):
        upper = (index & bit) != 0
        grown = {}
        for key, block in blocks.items():
            other = lax.ppermute(block, WIDE, [(i, i ^ bit) for i in range(8)])
            grown[key] = jnp.where(upper, other, block)
            grown[key | bit] = jnp.where(upper, block, other)
        blocks = grown
    return jnp.concatenate([blocks[key] for key in range(8)], axis=0)


owner_tree = {
    0: ([(3, 2), (1, 0)], [(2, 0)]),
    1: ([(0, 1), (3, 2)], [(2, 1)]),
    2: ([(3, 2), (0, 1)], [(1, 2)]),
    3: ([(0, 1), (2, 3)], [(1, 3)]),
}


def add_low(left, right):
    return (left.astype(jnp.float32) + right.astype(jnp.float32)).astype(left.dtype)


def tied(anchor, values):
    return lax.optimization_barrier((anchor, values))


def choose_owner(pieces):
    place = lax.axis_index("shard")
    own = pieces[0]
    for owner in range(1, len(pieces)):
        own = jnp.where(place == owner, pieces[owner], own)
    return own


def to_partner(values):
    return lax.ppermute(values, "core", [(0, 1), (1, 0)])


def paired(values):
    return jnp.concatenate([values, to_partner(values)], axis=0)


def split_rows(rows):
    return rows.reshape(rows.shape[0] // 16, 2, 8, rows.shape[1])


def one_parity(rows, parity):
    grouped = split_rows(rows)
    return lax.dynamic_index_in_dim(grouped, parity, axis=1, keepdims=False).reshape(
        rows.shape[0] // 2, rows.shape[1]
    )


ends_apart = [(0, 1), (1, 0), (2, 3), (3, 2)]
middle_pair = [(1, 2), (2, 1)]
outward = [(1, 0), (2, 3)]


def gather_rows(params, parity):
    count = params.shape[0] // 2
    place = lax.axis_index("shard")
    middle = (place == 1) | (place == 2)
    part = 2 * count // lax.axis_size("chip")
    piece = one_parity(
        lax.dynamic_slice_in_dim(params, lax.axis_index("chip") * part, part, axis=0), parity
    ).astype(jnp.bfloat16)

    def moved(values, pairs):
        return lax.ppermute(values, "shard", pairs)

    near = moved(piece, ends_apart)
    inner = moved(piece, middle_pair)
    crossed = moved(near, middle_pair)
    second = jnp.where(middle, inner, moved(inner, outward))
    third = jnp.where(middle, crossed, moved(crossed, outward))
    upper = place >= 2
    owners = (
        jnp.where(place % 2 == 0, place + 1, place - 1),
        jnp.where(upper, 1, 2),
        jnp.where(upper, 0, 3),
    )
    own = one_parity(lax.optimization_barrier(params), parity).astype(jnp.bfloat16)
    whole = lax.dynamic_update_slice_in_dim(
        jnp.zeros((4 * count, D), jnp.bfloat16), own, place * count, axis=0
    )
    for owner, rows in zip(owners, (near, second, third)):
        rows = lax.all_gather(rows, "chip", axis=0, tiled=True)
        whole = lax.dynamic_update_slice_in_dim(whole, rows, owner * count, axis=0)
    return whole


def adam_rows(place, block, grad_low, state, carried):
    groups = block // 8

    def rows_of(i, place_ref):
        return (place_ref[0] + (i // 2) * place_ref[1], i % 2, 0, 0)

    spec = pl.BlockSpec((pl.Element(groups), pl.Element(1), pl.Element(8), pl.Element(D)), rows_of)

    def body(place_ref, grad_ref, param_ref, first_ref, second_ref, *rest):
        out_refs = rest[-4:]
        grad = grad_ref[...].astype(jnp.float32).reshape(groups, 1, 8, D)
        param_new, first_new, second_new = adam_update(
            param_ref[...], grad, first_ref[...], second_ref[...], weight_decay
        )
        for ref, value in zip(out_refs, (grad, param_new, first_new, second_new)):
            ref[...] = value

    count = grad_low.shape[0]
    shape = jax.ShapeDtypeStruct(state[0].shape, jnp.float32)
    return pl.pallas_call(
        body,
        grid_spec=pltpu.PrefetchScalarGridSpec(
            num_scalar_prefetch=1,
            grid=(count // block,),
            in_specs=[pl.BlockSpec((block, D), lambda i, place_ref: (i, 0))]
            + [spec] * 3
            + [pl.BlockSpec(memory_space=pl.ANY)] * len(carried),
            out_specs=[spec] * 4,
        ),
        out_shape=[shape] * 4,
        input_output_aliases={5 + k: k for k in range(len(carried))},
        cost_estimate=pl.CostEstimate(
            flops=20 * count * D, transcendentals=count * D, bytes_accessed=30 * count * D
        ),
        compiler_params=pltpu.CompilerParams(vmem_limit_bytes=56 * 2**20),
        name="adam_rows",
    )(place, grad_low, *state, *carried)


def per_device(
    tokens, seg_ids, cotangent, params, gains, first_moment, second_moment, gain_first, gain_second
):
    wide_count = wide_size()
    shard_count = lax.axis_size("shard")
    tree = wide_count == 8 and shard_count == 4
    owner_rows = params.shape[0]
    total_rows = owner_rows * shard_count
    early_rows = (HEADS + 2 * KV_HEADS) * HD + HEADS * HD
    wide_index = lax.axis_index(WIDE)
    core_index = lax.axis_index("core")

    def own_slice(first, count):
        part = count // wide_count
        return lax.dynamic_slice_in_dim(
            params, first + wide_index * part, part, axis=0
        ).astype(jnp.bfloat16)

    if tree:
        rows_used = gather_rows(params, core_index)
        early_used = spread_first(own_slice(0, early_rows))
        split = 2
    else:
        rows_used = lax.all_gather(
            own_slice(0, owner_rows), ("shard",) + WIDE, axis=0, tiled=True
        )
        early_used = rows_used[:early_rows]
        split = 1
    gains_used = gather_columns(gains.astype(jnp.bfloat16), "shard")
    gains_float = gains_used.astype(jnp.float32)
    query_width = HEADS * HD
    kv_width = KV_HEADS * HD
    per_group = HEADS // KV_HEADS
    qkv_rows = query_width + 2 * kv_width
    out_end = qkv_rows + query_width
    gate_end = out_end + 2 * FF
    w_qkv = early_used[:qkv_rows]
    w_out = early_used[qkv_rows:out_end]
    gate_first, up_first, down_first, hidden_width = (
        out_end // split,
        (out_end + FF) // split,
        gate_end // split,
        FF // split,
    )
    w_gate_up = rows_used[gate_first:down_first]
    w_down = rows_used[down_first:]
    row_count = tokens.shape[0]
    block_rows = min(512, row_count)
    block_count = row_count // block_rows
    query_scale = HD ** (-0.5)
    inputs = tokens.astype(jnp.float32)
    cosine_table, sine_table = rotary_tables(positions_of(seg_ids), HD)
    normed, pull_first = jax.vjp(rms_scale, inputs, gains_float[0])
    normed_low = normed.astype(jnp.bfloat16)
    projected = times_transposed(normed_low, w_qkv)
    query_raw = projected[:, :query_width].reshape(row_count, HEADS, HD)
    key_raw = projected[:, query_width : query_width + kv_width].reshape(row_count, KV_HEADS, HD)
    value_heads = (
        projected[:, query_width + kv_width :].astype(jnp.bfloat16).reshape(row_count, KV_HEADS, HD)
    )
    queries = (rotate(query_raw, cosine_table, sine_table) * query_scale).astype(jnp.bfloat16)
    key_heads = rotate(key_raw, cosine_table, sine_table).astype(jnp.bfloat16)
    query_blocks = queries.reshape(block_count, block_rows, KV_HEADS, per_group, HD)
    segment_blocks = seg_ids.reshape(block_count, block_rows)
    block_starts = jnp.arange(block_count, dtype=jnp.int32) * block_rows

    def forward_block(inputs_block):
        query_block, segment_block, first_row = inputs_block
        scores = jnp.einsum(
            "qgnd,kgd->gnqk", query_block, key_heads, preferred_element_type=jnp.float32
        )
        capped = softcap_limit * jnp.tanh(scores / softcap_limit)
        allowed = block_mask(segment_block, seg_ids, first_row)
        row_top = jnp.max(jnp.where(allowed, capped, masked_floor), axis=-1, keepdims=True)
        weights_exp = jnp.where(allowed, jnp.exp(jnp.where(allowed, capped - row_top, 0.0)), 0.0)
        totals = jnp.sum(weights_exp, axis=-1, keepdims=True)
        probability = (weights_exp / totals).astype(jnp.bfloat16)
        mixed_block = jnp.einsum(
            "gnqk,kgd->qgnd", probability, value_heads, preferred_element_type=jnp.float32
        )
        return (mixed_block, row_top + jnp.log(totals))

    mixed_heads, log_totals = lax.map(forward_block, (query_blocks, segment_blocks, block_starts))
    mixed_low = mixed_heads.reshape(row_count, query_width).astype(jnp.bfloat16)
    attended = jnp.dot(mixed_low, w_out, preferred_element_type=jnp.float32)
    attn_normed, pull_second = jax.vjp(rms_scale, attended, gains_float[1])
    first_sum = inputs + attn_normed
    ffn_input, pull_third = jax.vjp(rms_scale, first_sum, gains_float[2])
    ffn_low = ffn_input.astype(jnp.bfloat16)
    if tree:
        ffn_low = paired(ffn_low)
    gate_up_kept = lax.optimization_barrier(
        times_transposed(ffn_low, w_gate_up).astype(jnp.bfloat16)
    )

    gate = gate_up_kept[:, :hidden_width].astype(jnp.float32)
    up = gate_up_kept[:, hidden_width:].astype(jnp.float32)
    active, pull_active = jax.vjp(lambda v: jax.nn.gelu(v, approximate=True), gate)
    gate_factor = (pull_active(jnp.ones_like(gate))[0] * up).astype(jnp.bfloat16)
    hidden = active * up
    hidden_low, gate_factor, up_factor = lax.optimization_barrier(
        (hidden.astype(jnp.bfloat16), gate_factor, active.astype(jnp.bfloat16))
    )
    if tree:
        other_branch = jnp.dot(
            hidden_low[row_count:], w_down, preferred_element_type=jnp.float32
        )
        hidden_low, other_branch = tied(hidden_low, other_branch)
        own_branch, other_branch = tied(
            jnp.dot(hidden_low[:row_count], w_down, preferred_element_type=jnp.float32),
            to_partner(other_branch),
        )
        branch = own_branch + other_branch
    else:
        branch = jnp.dot(hidden_low, w_down, preferred_element_type=jnp.float32)
    ffn_normed, pull_fifth = jax.vjp(rms_scale, branch, gains_float[3])
    result = first_sum + ffn_normed
    upstream = cotangent.astype(jnp.float32)
    branch_grad, gain_four = pull_fifth(upstream)
    branch_low = branch_grad.astype(jnp.bfloat16)
    if tree:
        branch_low = paired(branch_low)

    def product_rows(left, right):
        def rows(first, last):
            return contract_rows(left[:, first:last], right).astype(jnp.bfloat16)

        return rows

    factors = {
        "down": (down_first, total_rows // split, product_rows(hidden_low, branch_low))
    }
    steps = {}
    late_rows = early_rows // split
    segment_rows = owner_rows // split

    def bounds(key):
        return (max(key * segment_rows, late_rows), (key + 1) * segment_rows)

    def plane_terms(first, last):
        parts = [
            rows(max(first, start) - start, min(last, end) - start)
            for start, end, rows in sorted(factors.values(), key=lambda f: f[0])
            if max(first, start) < min(last, end)
        ]
        return parts[0] if len(parts) == 1 else jnp.concatenate(parts, axis=0)

    def start_ready(anchor, lowest):
        keys = [
            key
            for key in reversed(range(shard_count))
            if key not in steps and bounds(key)[0] >= lowest
        ]
        if not tree or not keys:
            return anchor
        terms = [plane_terms(*bounds(key)) for key in keys]
        for key, term in zip(keys, terms):
            steps[key] = [lax.psum_scatter(term, "chip", scatter_dimension=0, tiled=True)]
        return tied(anchor, terms)[0]

    def advance(key):
        pairs = owner_tree[max(key, 0)][len(steps[key]) - 1]
        held = steps[key][-1]
        moved = lax.ppermute(held, "shard", pairs)
        steps[key].append(add_low(held, moved))

    def tick(anchor, *keys):
        if not tree:
            return anchor
        anchor, values = tied(anchor, [steps[key][-1] for key in keys])
        for key, value in zip(keys, values):
            steps[key][-1] = value
            advance(key)
        return anchor

    branch_low = start_ready(branch_low, down_first)
    hidden_grad = times_transposed(branch_low, w_down)
    gate_grad = hidden_grad * gate_factor.astype(jnp.float32)
    up_grad = hidden_grad * up_factor.astype(jnp.float32)
    gate_low, up_low = gate_grad.astype(jnp.bfloat16), up_grad.astype(jnp.bfloat16)
    factors["gate"] = (gate_first, up_first, product_rows(gate_low, ffn_low))
    factors["up"] = (up_first, down_first, product_rows(up_low, ffn_low))
    gate_low, up_low = start_ready((gate_low, up_low), gate_first)
    gate_low, up_low = tick((gate_low, up_low), 3)

    def input_grad_of(first, last):
        return jnp.dot(
            gate_low[first:last], w_gate_up[:hidden_width], preferred_element_type=jnp.float32
        ) + jnp.dot(
            up_low[first:last], w_gate_up[hidden_width:], preferred_element_type=jnp.float32
        )

    if tree:
        other_grad = input_grad_of(row_count, 2 * row_count)
        (gate_low, up_low), other_grad = tied((gate_low, up_low), other_grad)
        ffn_input_grad = input_grad_of(0, row_count) + to_partner(other_grad)
    else:
        ffn_input_grad = input_grad_of(0, row_count)
    ffn_input_grad = tick(ffn_input_grad, 2)
    sum_grad_part, gain_three = pull_third(ffn_input_grad)
    sum_grad = upstream + sum_grad_part
    attended_grad, gain_two = pull_second(sum_grad)
    attended_low = attended_grad.astype(jnp.bfloat16)
    out_rows = product_rows(mixed_low, attended_low)

    factors["out"] = (qkv_rows // split, gate_first, out_rows)

    mixed_grad = (
        times_transposed(attended_low, w_out)
        .astype(jnp.bfloat16)
        .reshape(block_count, block_rows, KV_HEADS, per_group, HD)
    )

    mixed_grad = start_ready(mixed_grad, late_rows)
    mixed_grad = tick(mixed_grad, 3)

    def backward_block(running, inputs_block):
        key_acc, value_acc = running
        query_block, grad_block, segment_block, first_row, log_block = inputs_block
        scores = jnp.einsum(
            "qgnd,kgd->gnqk", query_block, key_heads, preferred_element_type=jnp.float32
        )
        capped = softcap_limit * jnp.tanh(scores / softcap_limit)
        allowed = block_mask(segment_block, seg_ids, first_row)
        probability = jnp.where(allowed, jnp.exp(jnp.where(allowed, capped - log_block, 0.0)), 0.0)
        probability_low = probability.astype(jnp.bfloat16)
        value_acc = value_acc + jnp.einsum(
            "gnqk,qgnd->kgd", probability_low, grad_block, preferred_element_type=jnp.float32
        )
        prob_grad = jnp.einsum(
            "qgnd,kgd->gnqk", grad_block, value_heads, preferred_element_type=jnp.float32
        )
        centred = jnp.sum(probability * prob_grad, axis=-1, keepdims=True)
        score_grad = (
            probability * (prob_grad - centred) * (1.0 - (capped / softcap_limit) ** 2)
        ).astype(jnp.bfloat16)
        query_grad_block = jnp.einsum(
            "gnqk,kgd->qgnd", score_grad, key_heads, preferred_element_type=jnp.float32
        )
        key_acc = key_acc + jnp.einsum(
            "gnqk,qgnd->kgd", score_grad, query_block, preferred_element_type=jnp.float32
        )
        return ((key_acc, value_acc), query_grad_block)

    zero_heads = jnp.zeros((row_count, KV_HEADS, HD), jnp.float32)
    (key_grad, value_grad), query_grad = lax.scan(
        backward_block,
        (zero_heads, zero_heads),
        (query_blocks, mixed_grad, segment_blocks, block_starts, log_totals),
    )
    query_grad = tick(query_grad, 2, 1)
    query_raw_grad = rotate(
        query_grad.reshape(row_count, HEADS, HD) * query_scale, cosine_table, -sine_table
    )
    key_raw_grad = rotate(key_grad, cosine_table, -sine_table)
    qkv_low = jnp.concatenate(
        [
            query_raw_grad.reshape(row_count, query_width),
            key_raw_grad.reshape(row_count, kv_width),
            value_grad.reshape(row_count, kv_width),
        ],
        axis=1,
    ).astype(jnp.bfloat16)
    factors["qkv"] = (0, qkv_rows // split, product_rows(qkv_low, normed_low))
    normed_grad = jnp.dot(qkv_low, w_qkv, preferred_element_type=jnp.float32)
    input_part, gain_one = pull_first(normed_grad)
    input_grad = sum_grad + input_part
    state = (params, first_moment, second_moment)
    if tree:
        qkv_grad = product_rows(qkv_low, normed_low)(0, qkv_rows)
        late_grad = jnp.concatenate([qkv_grad, out_rows(0, query_width)], axis=0)
        by_piece = (
            late_grad.reshape(wide_count // 2, -1, 2, 8, D)
            .transpose(0, 2, 1, 3, 4)
            .reshape(early_rows, D)
        )
        steps[-1] = [lax.psum_scatter(by_piece, WIDE, scatter_dimension=0, tiled=True)]
        for key in (3, 2, 1, 0, -1):
            while len(steps[key]) < 3:
                advance(key)
        late_part = early_rows // wide_count
        early_part = owner_rows // wide_count - late_part
        whole_pieces = [steps[owner][-1] for owner in range(1, shard_count)]
        early_piece = choose_owner([steps[0][-1]] + [p[:early_part] for p in whole_pieces])
        late_piece = choose_owner([steps[-1][-1]] + [p[early_part:] for p in whole_pieces])
        first_owner = lax.axis_index("shard") == 0
        early_groups, late_groups = early_part // 8, late_part // 8
        early_place = jnp.where(
            first_owner,
            jnp.array([early_rows // 16, early_groups], jnp.int32),
            jnp.array([0, early_groups + late_groups], jnp.int32),
        )
        late_place = jnp.where(
            first_owner,
            jnp.array([0, late_groups], jnp.int32),
            jnp.array([early_groups, early_groups + late_groups], jnp.int32),
        )
        early_low = lax.all_gather(early_piece, WIDE, axis=0, tiled=True)
        late_low = lax.all_gather(late_piece, WIDE, axis=0, tiled=True)
        state = [split_rows(rows) for rows in (params, first_moment, second_moment)]
        carried = adam_rows(early_place, early_part, early_low, state, ())
        row_grad, new_params, new_first, new_second = [
            rows.reshape(owner_rows, D)
            for rows in adam_rows(late_place, late_part, late_low, state, carried)
        ]
    else:
        own = lax.psum_scatter(
            plane_terms(0, total_rows), ("shard",) + WIDE, scatter_dimension=0, tiled=True
        )
        row_grad = lax.all_gather(own, WIDE, axis=0, tiled=True).astype(jnp.float32)
        new_params, new_first, new_second = adam_update(
            params, row_grad, first_moment, second_moment, weight_decay
        )
    gain_terms = jnp.stack([gain_one, gain_two, gain_three, gain_four])
    gain_total = butterfly_sum(
        butterfly_sum(gain_terms, WIDE, wide_count), "shard", shard_count
    )
    gain_grad = lax.dynamic_slice_in_dim(
        gain_total, lax.axis_index("shard") * gains.shape[1], gains.shape[1], axis=1
    )
    new_gains, new_gain_first, new_gain_second = adam_update(
        gains, gain_grad, gain_first, gain_second, 0.0
    )
    return (
        result.astype(jnp.bfloat16),
        input_grad.astype(jnp.bfloat16),
        row_grad,
        gain_grad,
        new_params,
        new_gains,
        new_first,
        new_second,
        new_gain_first,
        new_gain_second,
    )


def solution(mesh):
    wide = mesh.shape["wide"]

    split_mesh = Mesh(
        mesh.devices.reshape(wide // 2, 2, mesh.shape["shard"]),
        ("chip", "core", "shard"),
    )
    return jax.shard_map(
        per_device,
        mesh=split_mesh,
        in_specs=(
            P(("chip", "core", "shard"), None),
            P(("chip", "core", "shard")),
            P(("chip", "core", "shard"), None),
            P("shard", None),
            P(None, "shard"),
            P("shard", None),
            P("shard", None),
            P(None, "shard"),
            P(None, "shard"),
        ),
        out_specs=(
            P(("chip", "core", "shard"), None),
            P(("chip", "core", "shard"), None),
            P("shard", None),
            P(None, "shard"),
            P("shard", None),
            P(None, "shard"),
            P("shard", None),
            P("shard", None),
            P(None, "shard"),
            P(None, "shard"),
        ),
        check_vma=False,
    )
```

profile of v0, /device:TPU:0, one launch (start us, length us, event | category | flops | bytes accessed | tf_op | source)
XLA Modules:
  0.0 1077.9 jit_solution(7312431106974497316)
XLA Ops:
  14.9 36.7 %collective-permute-done.13 = bf16[728,1152]{1,0:T(8,128)(2,1)} collective-permute-done((bf16[728,1152]{1,0:T(8,128)(2,1)S(1)}, bf16[728,1152]{1,0:T(8,128)(2,1)}, u32[]{:S(2)}, u32[]{:S(2)}) %collective-permute-start.13) | collective-permute-done | bytes 1677344 | tf_op jit(solution)/shard_map/ppermute | solution.py:211
  62.4 12.5 %collective-permute-done.3 = bf16[320,1152]{1,0:T(8,128)(2,1)} collective-permute-done((bf16[320,1152]{1,0:T(8,128)(2,1)S(1)}, bf16[320,1152]{1,0:T(8,128)(2,1)}, u32[]{:S(2)}, u32[]{:S(2)}) %collective-permute-start.3) | collective-permute-done | bytes 737312 | tf_op jit(solution)/shard_map/ppermute | solution.py:136
  76.4 38.7 %collective-permute-start.4 = (bf16[320,1152]{1,0:T(8,128)(2,1)S(1)}, bf16[320,1152]{1,0:T(8,128)(2,1)}, u32[]{:S(2)}, u32[]{:S(2)}) collective-permute-start(bf16[320,1152]{1,0:T(8,128)(2,1)S(1)} %broadcast_select_fusion.2), channel_id=1, source_target_pairs={{0,1},{2,3},{4,5},{6,7},{8,9},{10,11},{12,13},{14,15},{16,17},{18,... | collective-permute-start | bytes 2211848 | tf_op jit(solution)/shard_map/ppermute | solution.py:138
  118.2 10.1 collective-permute-done.4
  131.1 13.6 %collective-permute-done.15 = bf16[728,1152]{1,0:T(8,128)(2,1)} collective-permute-done((bf16[728,1152]{1,0:T(8,128)(2,1)}, bf16[728,1152]{1,0:T(8,128)(2,1)}, u32[]{:S(2)}, u32[]{:S(2)}) %collective-permute-start.15) | collective-permute-done | bytes 1677344 | tf_op jit(solution)/shard_map/ppermute | solution.py:211
  176.5 20.2 %collective-permute-done.6 = bf16[320,1152]{1,0:T(8,128)(2,1)} collective-permute-done((bf16[320,1152]{1,0:T(8,128)(2,1)}, bf16[320,1152]{1,0:T(8,128)(2,1)}, u32[]{:S(2)}, u32[]{:S(2)}) %collective-permute-start.6) | collective-permute-done | bytes 737312 | tf_op jit(solution)/shard_map/ppermute | solution.py:146
  199.0 19.2 %collective-permute-start.2 = (bf16[4,288]{1,0:T(4,128)(2,1)S(1)}, bf16[4,288]{1,0:T(4,128)(2,1)S(1)}, u32[]{:S(2)}, u32[]{:S(2)}) collective-permute-start(bf16[4,288]{1,0:T(4,128)(2,1)S(1)} %convert_element_type.242), channel_id=1, source_target_pairs={{0,3},{1,0},{2,1},{3,2},{4,7},{5,4},{6,5},{7,6},{8,11},{9,8},{10,9... | collective-permute-start | bytes 6920 | tf_op jit(solution)/shard_map/ppermute | solution.py:128
  253.7 17.7 %collective-permute-done.17 = bf16[728,1152]{1,0:T(8,128)(2,1)} collective-permute-done((bf16[728,1152]{1,0:T(8,128)(2,1)}, bf16[728,1152]{1,0:T(8,128)(2,1)}, u32[]{:S(2)}, u32[]{:S(2)}) %collective-permute-start.17) | collective-permute-done | bytes 1677344 | tf_op jit(solution)/shard_map/ppermute | solution.py:211
  274.5 27.0 %while.31 = (s32[]{:T(128)}, bf16[2,512,1,4,256]{4,1,3,2,0:T(8,128)(2,1)}, f32[2,1,4,512,1]{3,2,4,1,0:T(4,128)S(1)}, s32[2,512]{1,0:T(2,128)S(1)}, s32[1024]{0:T...) while((s32[]{:T(128)}, ...), condition=%wide.region_6.7_spmd.clone, body=%wide.region_3.6_spmd.sunk.clone | while | flops 2186279424 | bytes 50411736 | solution.py:355
  330.3 27.2 %all-gather.10.cloned.1.call-done = bf16[2912,1152]{1,0:T(8,128)(2,1)} async-done(((bf16[728,1152]{1,0:T(8,128)(2,1)}), bf16[2912,1152]{1,0:T(8,128)(2,1)}) %all-gather.10.cloned.1.call-update) | async-done | bytes 6709264 | tf_op jit(solution)/shard_map/all_gather | solution.py:229
  363.7 45.1 %convolution_convert_fusion = bf16[2048,6912]{1,0:T(8,128)(2,1)} fusion(bf16[11648,1152]{1,0:T(8,128)(2,1)} %constant_dynamic-update-slice_fusion.1, bf16[1024,1152]{1,0:T(8,128)(2,1)} %collective-permute-done.12, bf16[1024,1152]{1,0:T(8,128)(2,1)S(1)} %multiply_convert_fusion.2), kind=kOutput, calls=%fused_computation.94 | convolution fusion | flops 32638500864 | bytes 48955392 | tf_op jit(solution)/shard_map/dot_general | solution.py:74
  408.9 32.1 %fusion.75 = (bf16[2048,3456]{1,0:T(8,128)(2,1)}, bf16[2048,3456]{1,0:T(8,128)(2,1)}, bf16[2048,3456]{1,0:T(8,128)(2,1)}) fusion(bf16[2048,6912]{1,0:T(8,128)(2,1)} %convolution_convert_fusion), kind=kLoop, calls=%fused_computation.95 | loop fusion | flops 176947200 | bytes 70778880 | tf_op jit(solution)/shard_map/convert_element_type | solution.py:374
  441.0 15.8 %fusion.98 = f32[1024,1152]{1,0:T(8,128)} fusion(bf16[2048,3456]{1,0:T(8,128)(2,1)} %get-tuple-element.242, bf16[11648,1152]{1,0:T(8,128)(2,1)} %constant_dynamic-update-slice_fusion.1), kind=kOutput, calls=%fused_computation.124 | convolution fusion | flops 8153726976 | bytes 19759104 | tf_op jit(solution)/shard_map/dot_general | solution.py:377
  456.8 14.5 %fusion.96 = f32[1024,1152]{1,0:T(8,128)} fusion(bf16[2048,3456]{1,0:T(8,128)(2,1)S(1)} %copy-done.13, bf16[11648,1152]{1,0:T(8,128)(2,1)} %constant_dynamic-update-slice_fusion.1), kind=kOutput, calls=%fused_computation.122 | convolution fusion | flops 8153726976 | bytes 19759104 | tf_op jit(solution)/shard_map/dot_general | solution.py:382
  485.2 22.4 %fusion.79 = bf16[2912,1152]{1,0:T(8,128)(2,1)} fusion(bf16[2048,3456]{1,0:T(8,128)(2,1)} %get-tuple-element.242, bf16[1024,1152]{1,0:T(8,128)(2,1)S(1)} %collective-permute-done.19, bf16[1024,1152]{1,0:T(8,128)(2,1)S(1)} %get-tuple-element.468), kind=kOutput, calls=%fused_computation.100 | convolution fusion | flops 13753331712 | bytes 23486464 | tf_op jit(solution)/shard_map/dot_general | solution.py:68
  517.9 31.9 %multiply_convert_fusion = (bf16[2048,3456]{1,0:T(8,128)(2,1)}, bf16[2048,3456]{1,0:T(8,128)(2,1)}) fusion(bf16[2048,3456]{1,0:T(8,128)(2,1)} %get-tuple-element.248, bf16[2048,3456]{1,0:T(8,128)(2,1)} %get-tuple-element.247, bf16[2048,1152]{1,0:T(8,128)(2,1)} %pad_maximum_fusion.4, bf16[11648,1152]{1,0:T(8,128)(2,1)} %constant_dynamic-update-slice_fusion.1), kind=kOutput, calls=%fused_computation.92 | convolution fusion | flops 16349921280 | bytes 69304320 | tf_op jit(solution)/shard_map/dot_general | solution.py:74
  549.8 20.1 %convolution_convert_fusion.1 = bf16[2368,1152]{1,0:T(8,128)(2,1)} fusion(bf16[2048,3456]{1,0:T(8,128)(2,1)} %get-tuple-element.254, bf16[1024,1152]{1,0:T(8,128)(2,1)} %collective-permute-done.12, bf16[1024,1152]{1,0:T(8,128)(2,1)S(1)} %copy-done.28), kind=kOutput, calls=%fused_computation.101 | convolution fusion | flops 11185790976 | bytes 20135936 | tf_op jit(solution)/shard_map/dot_general | solution.py:68
  576.0 9.9 convolution_convert_fusion.4
  586.0 14.5 %fusion.85 = bf16[1824,1152]{1,0:T(8,128)(2,1)S(1)} fusion(bf16[2048,3456]{1,0:T(8,128)(2,1)} %get-tuple-element.253, bf16[1024,1152]{1,0:T(8,128)(2,1)} %collective-permute-done.12, bf16[1024,1152]{1,0:T(8,128)(2,1)S(1)} %copy-done.29), kind=kOutput, calls=%fused_computation.111 | convolution fusion | flops 8618250240 | bytes 16785408 | tf_op jit(solution)/shard_map/dot_general | solution.py:68
  605.5 14.5 %convolution_convert_fusion.3 = bf16[1632,1152]{1,0:T(8,128)(2,1)} fusion(bf16[2048,3456]{1,0:T(8,128)(2,1)} %get-tuple-element.253, bf16[1024,1152]{1,0:T(8,128)(2,1)} %collective-permute-done.12, bf16[1024,1152]{1,0:T(8,128)(2,1)S(1)} %copy-done.30), kind=kOutput, calls=%fused_computation.112 | convolution fusion | flops 7712059392 | bytes 15294464 | tf_op jit(solution)/shard_map/dot_general | solution.py:68
  620.1 13.2 %fusion.92 = f32[1024,1152]{1,0:T(8,128)S(1)} fusion(bf16[2048,3456]{1,0:T(8,128)(2,1)} %get-tuple-element.254, bf16[11648,1152]{1,0:T(8,128)(2,1)} %constant_dynamic-update-slice_fusion.1), kind=kOutput, calls=%fused_computation.118 | convolution fusion | flops 8153726976 | bytes 19759104 | tf_op jit(solution)/shard_map/dot_general | solution.py:461
  633.3 16.8 %fusion.115 = f32[1024,1152]{1,0:T(8,128)} fusion(f32[1024,1152]{1,0:T(8,128)S(1)} %fusion.92, bf16[11648,1152]{1,0:T(8,128)(2,1)} %constant_dynamic-update-slice_fusion.1, bf16[2048,3456]{1,0:T(8,128)(2,1)} %get-tuple-element.253), kind=kOutput, calls=%fused_computation.151 | convolution fusion | flops 8154906624 | bytes 24477696 | tf_op jit(solution)/shard_map/dot_general | solution.py:459
  656.6 13.4 %fusion.88 = f32[1024,1152]{1,0:T(8,128)S(1)} fusion(bf16[2048,3456]{1,0:T(8,128)(2,1)} %get-tuple-element.254, bf16[11648,1152]{1,0:T(8,128)(2,1)} %constant_dynamic-update-slice_fusion.1), kind=kOutput, calls=%fused_computation.114 | convolution fusion | flops 8153726976 | bytes 19759104 | tf_op jit(solution)/shard_map/dot_general | solution.py:461
  670.0 22.1 %collective-permute-done.21 = bf16[728,1152]{1,0:T(8,128)(2,1)S(1)} collective-permute-done((bf16[728,1152]{1,0:T(8,128)(2,1)S(1)}, bf16[728,1152]{1,0:T(8,128)(2,1)S(1)}, u32[]{:S(2)}, u32[]{:S(2)}) %collective-permute-start.21) | collective-permute-done | bytes 1677344 | tf_op jit(solution)/shard_map/ppermute | solution.py:436
  693.7 16.5 %fusion.125 = f32[1024,1152]{1,0:T(8,128)} fusion(f32[1024,1152]{1,0:T(8,128)} %collective-permute-done.20, f32[1024,1152]{1,0:T(8,128)S(1)} %fusion.88, bf16[11648,1152]{1,0:T(8,128)(2,1)} %constant_dynamic-update-slice_fusion.1, bf16[2048,3456]{1,0:T(8,128)(2,1)} %get-tuple-element.253), kind=kOutput, calls=%fused_computation.153 | convolution fusion | flops 8156086272 | bytes 29196288 | tf_op jit(solution)/shard_map/dot_general | solution.py:459
  743.0 49.3 %while.32 = (s32[]{:T(128)}, f32[1024,1,256]{0,2,1:T(8,128)S(1)}, f32[1024,1,256]{0,2,1:T(8,128)}, f32[2,512,1,4,256]{4,1,3,2,0:T(8,128)}, bf16[2,512,1,4,256]{4...) while((s32[]{:T(128)}, f32[1024,1,256]{0,2,1:T(8,128)S(1)}, ...), condition=%wide.region_17.18_spmd.clone.clone, body=%wide.region_15.17_spmd.clone.sunk.clone | while | flops 5423233536 | bytes 125376864 | solution.py:518
  834.3 30.2 %collective-permute-done.25 = bf16[728,1152]{1,0:T(8,128)(2,1)} collective-permute-done((bf16[728,1152]{1,0:T(8,128)(2,1)}, bf16[728,1152]{1,0:T(8,128)(2,1)}, u32[]{:S(2)}, u32[]{:S(2)}) %collective-permute-start.25) | collective-permute-done | bytes 1677344 | tf_op jit(solution)/shard_map/ppermute | solution.py:436
  873.8 54.2 %collective-permute-done.30 = bf16[408,1152]{1,0:T(8,128)(2,1)S(1)} collective-permute-done((bf16[408,1152]{1,0:T(8,128)(2,1)S(1)}, bf16[408,1152]{1,0:T(8,128)(2,1)S(1)}, u32[]{:S(2)}, u32[]{:S(2)}) %collective-permute-start.30) | collective-permute-done | bytes 940064 | tf_op jit(solution)/shard_map/ppermute | solution.py:436
  930.9 16.7 %collective-permute-done.27 = bf16[320,1152]{1,0:T(8,128)(2,1)S(1)} collective-permute-done((bf16[320,1152]{1,0:T(8,128)(2,1)}, bf16[320,1152]{1,0:T(8,128)(2,1)S(1)}, u32[]{:S(2)}, u32[]{:S(2)}) %collective-permute-start.27) | collective-permute-done | bytes 737312 | tf_op jit(solution)/shard_map/ppermute | solution.py:436
  950.2 16.6 %collective-permute-done.28 = bf16[320,1152]{1,0:T(8,128)(2,1)S(1)} collective-permute-done((bf16[320,1152]{1,0:T(8,128)(2,1)S(1)}, bf16[320,1152]{1,0:T(8,128)(2,1)S(1)}, u32[]{:S(2)}, u32[]{:S(2)}) %collective-permute-start.28) | collective-permute-done | bytes 737312 | tf_op jit(solution)/shard_map/ppermute | solution.py:436
  996.4 41.1 %adam_rows.2 = (f32[364,2,8,1152]{3,2,1,0:T(8,128)}, f32[364,2,8,1152]{3,2,1,0:T(8,128)}, f32[364,2,8,1152]{3,2,1,0:T(8,128)}, f32[364,2,8,1152]{3,2,1,0:T(8,128)}) custom-call(s32[2]{0:T(128)} %broadcast_select_fusion.14.place_ref, bf16[3264,1152]{1,0:T(8,128)(2,1)} %all-gather.14.cloned.1.call-done.grad_ref, f32[364,2,8,1152]{3,2,1,0:T(8,128)} %bitcast.317, ...), custom_call_target="tpu_custom_call" | custom-call | flops 75202560 | bytes 112803840 | tf_op jit(solution)/shard_map/adam_rows/pallas_call | solution.py:253
  1037.5 33.4 %adam_rows.3 = (f32[364,2,8,1152]{3,2,1,0:T(8,128)}, f32[364,2,8,1152]{3,2,1,0:T(8,128)}, f32[364,2,8,1152]{3,2,1,0:T(8,128)}, f32[364,2,8,1152]{3,2,1,0:T(8,128)}) custom-call(s32[2]{0:T(128)} %broadcast_select_fusion.15.place_ref, ...), custom_call_target="tpu_custom_call", output_to_operand_aliasing={{0}: (5, {}), {1}: (6, {}), {2}: (7, {}), {3}: (8, {})} | custom-call | flops 58982400 | bytes 88473600 | tf_op jit(solution)/shard_map/adam_rows/pallas_call | solution.py:253
  (476 shorter events, 369.5 us)
Async XLA Ops:
  7.2 309.2 %all-gather.6.cloned.1.call-start = ((), (), s32[]{:S(2)}) async-start(), calls=%async_computation.5 | async-start | bytes 8386560 | tf_op jit(solution)/shard_map/all_gather | solution.py:229
  11.8 39.8 %collective-permute-start.13 = (bf16[728,1152]{1,0:T(8,128)(2,1)S(1)}, bf16[728,1152]{1,0:T(8,128)(2,1)}, u32[]{:S(2)}, u32[]{:S(2)}) collective-permute-start(bf16[728,1152]{1,0:T(8,128)(2,1)S(1)} %fusion.147), channel_id=1, source_target_pairs={{0,1},{1,0},{2,3},{3,2},{4,5},{5,4},{6,7},{7,6},{8,9},{9,8},{10,11... | collective-permute-start | bytes 5031944 | tf_op jit(solution)/shard_map/ppermute | solution.py:211
  51.7 272.4 %all-gather.8.cloned.1.call-start = ((), (), s32[]{:S(2)}) async-start(), calls=%async_computation.6 | async-start | bytes 8386560 | tf_op jit(solution)/shard_map/all_gather | solution.py:229
  61.1 83.6 %collective-permute-start.15 = (bf16[728,1152]{1,0:T(8,128)(2,1)}, bf16[728,1152]{1,0:T(8,128)(2,1)}, u32[]{:S(2)}, u32[]{:S(2)}) collective-permute-start(bf16[728,1152]{1,0:T(8,128)(2,1)} %collective-permute-done.14), channel_id=1, source_target_pairs={{1,0},{2,3},{5,4},{6,7},{9,8},{10,11},{13,12},{14,15},{17,16},{18,... | collective-permute-start | bytes 5031944 | tf_op jit(solution)/shard_map/ppermute | solution.py:211
  76.4 51.9 %collective-permute-start.4 = (bf16[320,1152]{1,0:T(8,128)(2,1)S(1)}, bf16[320,1152]{1,0:T(8,128)(2,1)}, u32[]{:S(2)}, u32[]{:S(2)}) collective-permute-start(bf16[320,1152]{1,0:T(8,128)(2,1)S(1)} %broadcast_select_fusion.2), channel_id=1, source_target_pairs={{0,1},{2,3},{4,5},{6,7},{8,9},{10,11},{12,13},{14,15},{16,17},{18,... | collective-permute-start | bytes 2211848 | tf_op jit(solution)/shard_map/ppermute | solution.py:138
  115.1 103.5 %collective-permute-start.1 = (bf16[4,288]{1,0:T(4,128)(2,1)S(1)}, bf16[4,288]{1,0:T(4,128)(2,1)S(1)}, u32[]{:S(2)}, u32[]{:S(2)}) collective-permute-start(bf16[4,288]{1,0:T(4,128)(2,1)S(1)} %convert_element_type.242), channel_id=1, source_target_pairs={{0,2},{1,3},{2,0},{3,1},{4,6},{5,7},{6,4},{7,5},{8,10},{9,11},{10,... | collective-permute-start | bytes 6920 | tf_op jit(solution)/shard_map/ppermute | solution.py:128
  116.4 82.6 %collective-permute-start = (bf16[4,288]{1,0:T(4,128)(2,1)S(1)}, bf16[4,288]{1,0:T(4,128)(2,1)S(1)}, u32[]{:S(2)}, u32[]{:S(2)}) collective-permute-start(bf16[4,288]{1,0:T(4,128)(2,1)S(1)} %convert_element_type.242), channel_id=1, source_target_pairs={{0,1},{1,2},{2,3},{3,0},{4,5},{5,6},{6,7},{7,4},{8,9},{9,10},{10,1... | collective-permute-start | bytes 6920 | tf_op jit(solution)/shard_map/ppermute | solution.py:128
  129.5 35.5 %collective-permute-start.5 = (bf16[320,1152]{1,0:T(8,128)(2,1)S(1)}, bf16[320,1152]{1,0:T(8,128)(2,1)}, u32[]{:S(2)}, u32[]{:S(2)}) collective-permute-start(bf16[320,1152]{1,0:T(8,128)(2,1)S(1)} %broadcast_select_fusion.3), channel_id=1, source_target_pairs={{0,16},{4,20},{8,24},{12,28},{16,0},{20,4},{24,8},{28,12},{1,17},{... | collective-permute-start | bytes 2211848 | tf_op jit(solution)/shard_map/ppermute | solution.py:146
  147.5 209.9 %all-gather.10.cloned.1.call-start = ((), (), s32[]{:S(2)}) async-start(), calls=%async_computation.7 | async-start | bytes 8386560 | tf_op jit(solution)/shard_map/all_gather | solution.py:229
  167.4 29.3 %collective-permute-start.6 = (bf16[320,1152]{1,0:T(8,128)(2,1)}, bf16[320,1152]{1,0:T(8,128)(2,1)}, u32[]{:S(2)}, u32[]{:S(2)}) collective-permute-start(bf16[320,1152]{1,0:T(8,128)(2,1)} %get-tuple-element.478), channel_id=1, source_target_pairs={{0,8},{4,12},{8,0},{12,4},{16,24},{20,28},{24,16},{28,20},{1,9},{5... | collective-permute-start | bytes 2211848 | tf_op jit(solution)/shard_map/ppermute | solution.py:146
  170.9 52.3 %collective-permute-start.16 = (bf16[728,1152]{1,0:T(8,128)(2,1)}, bf16[728,1152]{1,0:T(8,128)(2,1)}, u32[]{:S(2)}, u32[]{:S(2)}) collective-permute-start(bf16[728,1152]{1,0:T(8,128)(2,1)} %collective-permute-done.13), channel_id=1, source_target_pairs={{1,2},{2,1},{5,6},{6,5},{9,10},{10,9},{13,14},{14,13},{17,18},{18,... | collective-permute-start | bytes 5031944 | tf_op jit(solution)/shard_map/ppermute | solution.py:211
  175.9 44.4 %collective-permute-start.9 = (bf16[320,1152]{1,0:T(8,128)(2,1)}, bf16[320,1152]{1,0:T(8,128)(2,1)}, u32[]{:S(2)}, u32[]{:S(2)}) collective-permute-start(bf16[320,1152]{1,0:T(8,128)(2,1)} %get-tuple-element.477), channel_id=1, source_target_pairs={{0,8},{4,12},{8,0},{12,4},{16,24},{20,28},{24,16},{28,20},{1,9},{5... | collective-permute-start | bytes 2211848 | tf_op jit(solution)/shard_map/ppermute | solution.py:146
  199.0 25.7 %collective-permute-start.7 = (bf16[320,1152]{1,0:T(8,128)(2,1)}, bf16[320,1152]{1,0:T(8,128)(2,1)}, u32[]{:S(2)}, u32[]{:S(2)}) collective-permute-start(bf16[320,1152]{1,0:T(8,128)(2,1)} %get-tuple-element.480), channel_id=1, source_target_pairs={{0,4},{4,0},{8,12},{12,8},{16,20},{20,16},{24,28},{28,24},{1,5},{5... | collective-permute-start | bytes 2211848 | tf_op jit(solution)/shard_map/ppermute | solution.py:146
  199.0 20.5 %collective-permute-start.2 = (bf16[4,288]{1,0:T(4,128)(2,1)S(1)}, bf16[4,288]{1,0:T(4,128)(2,1)S(1)}, u32[]{:S(2)}, u32[]{:S(2)}) collective-permute-start(bf16[4,288]{1,0:T(4,128)(2,1)S(1)} %convert_element_type.242), channel_id=1, source_target_pairs={{0,3},{1,0},{2,1},{3,2},{4,7},{5,4},{6,5},{7,6},{8,11},{9,8},{10,9... | collective-permute-start | bytes 6920 | tf_op jit(solution)/shard_map/ppermute | solution.py:128
  222.7 83.5 %collective-permute-start.11 = (bf16[320,1152]{1,0:T(8,128)(2,1)}, bf16[320,1152]{1,0:T(8,128)(2,1)}, u32[]{:S(2)}, u32[]{:S(2)}) collective-permute-start(bf16[320,1152]{1,0:T(8,128)(2,1)} %get-tuple-element.475), channel_id=1, source_target_pairs={{0,4},{4,0},{8,12},{12,8},{16,20},{20,16},{24,28},{28,24},{1,5},{5... | collective-permute-start | bytes 2211848 | tf_op jit(solution)/shard_map/ppermute | solution.py:146
  223.2 48.2 %collective-permute-start.17 = (bf16[728,1152]{1,0:T(8,128)(2,1)}, bf16[728,1152]{1,0:T(8,128)(2,1)}, u32[]{:S(2)}, u32[]{:S(2)}) collective-permute-start(bf16[728,1152]{1,0:T(8,128)(2,1)} %collective-permute-done.16), channel_id=1, source_target_pairs={{1,0},{2,3},{5,4},{6,7},{9,8},{10,11},{13,12},{14,15},{17,16},{18,... | collective-permute-start | bytes 5031944 | tf_op jit(solution)/shard_map/ppermute | solution.py:211
  274.2 345.8 %reduce-scatter.16.cloned.1.call-start = ((), (), s32[]{:S(2)}) async-start(), calls=%async_computation.11 | async-start | bytes 8386560
  316.3 47.4 %collective-permute-start.12 = (bf16[1024,1152]{1,0:T(8,128)(2,1)S(1)}, bf16[1024,1152]{1,0:T(8,128)(2,1)}, u32[]{:S(2)}, u32[]{:S(2)}) collective-permute-start(bf16[1024,1152]{1,0:T(8,128)(2,1)S(1)} %multiply_convert_fusion.2), channel_id=1, source_target_pairs={{0,4},{4,0},{1,5},{5,1},{2,6},{6,2},{3,7},{7,3},{8,12},{12,8},{9,1... | collective-permute-start | bytes 7077896 | tf_op jit(solution)/shard_map/ppermute | solution.py:178
  507.6 202.7 %reduce-scatter.18.cloned.1.call-start = ((), (), s32[]{:S(2)}) async-start(), calls=%async_computation.12 | async-start | bytes 8386560
  575.8 231.5 %reduce-scatter.20.cloned.1.call-start = ((), (), s32[]{:S(2)}) async-start(), calls=%async_computation.13 | async-start | bytes 8386560
  603.9 228.2 %reduce-scatter.22.cloned.1.call-start = ((), (), s32[]{:S(2)}) async-start(), calls=%async_computation.14 | async-start | bytes 4700160
  650.1 43.6 %collective-permute-start.20 = (f32[1024,1152]{1,0:T(8,128)}, f32[1024,1152]{1,0:T(8,128)}, u32[]{:S(2)}, u32[]{:S(2)}) collective-permute-start(f32[1024,1152]{1,0:T(8,128)} %fusion.115), channel_id=1, source_target_pairs={{0,4},{4,0},{1,5},{5,1},{2,6},{6,2},{3,7},{7,3},{8,12},{12,8},{9,1... | collective-permute-start | bytes 14155784 | tf_op jit(solution)/shard_map/ppermute | solution.py:178
  652.5 277.0 %reduce-scatter.14.cloned.1.call-start = ((), (), s32[]{:S(2)}) async-start(), calls=%async_computation.8 | async-start | bytes 6635520 | tf_op jit(solution)/shard_map/reduce_scatter | solution.py:549
  652.6 39.5 %collective-permute-start.21 = (bf16[728,1152]{1,0:T(8,128)(2,1)S(1)}, bf16[728,1152]{1,0:T(8,128)(2,1)S(1)}, u32[]{:S(2)}, u32[]{:S(2)}) collective-permute-start(bf16[728,1152]{1,0:T(8,128)(2,1)S(1)} %copy-done.39), channel_id=1, source_target_pairs={{0,1},{2,3},{4,5},{6,7},{8,9},{10,11},{12,13},{14,15},{16,17},{18,... | collective-permute-start | bytes 5031944 | tf_op jit(solution)/shard_map/ppermute | solution.py:436
  737.5 66.7 %collective-permute-start.22 = (bf16[728,1152]{1,0:T(8,128)(2,1)}, bf16[728,1152]{1,0:T(8,128)(2,1)}, u32[]{:S(2)}, u32[]{:S(2)}) collective-permute-start(bf16[728,1152]{1,0:T(8,128)(2,1)} %reduce-scatter.18.cloned.1.call-done), channel_id=1, source_target_pairs={{3,2},{0,1},{7,6},{4,5},{11,10},{8,9},{15,14},{12,13},{19,18},{16,... | collective-permute-start | bytes 5031944 | tf_op jit(solution)/shard_map/ppermute | solution.py:436
  827.7 168.6 %all-gather.14.cloned.1.call-start = ((), (), s32[]{:S(2)}) async-start(), calls=%async_computation.10 | async-start | bytes 8460288 | tf_op jit(solution)/shard_map/all_gather | solution.py:570
  827.8 36.8 %collective-permute-start.25 = (bf16[728,1152]{1,0:T(8,128)(2,1)}, bf16[728,1152]{1,0:T(8,128)(2,1)}, u32[]{:S(2)}, u32[]{:S(2)}) collective-permute-start(bf16[728,1152]{1,0:T(8,128)(2,1)} %reduce-scatter.20.cloned.1.call-done), channel_id=1, source_target_pairs={{0,1},{3,2},{4,5},{7,6},{8,9},{11,10},{12,13},{15,14},{16,17},{19,... | collective-permute-start | bytes 5031944 | tf_op jit(solution)/shard_map/ppermute | solution.py:436
  830.3 40.6 %collective-permute-start.23 = (bf16[728,1152]{1,0:T(8,128)(2,1)}, bf16[728,1152]{1,0:T(8,128)(2,1)}, u32[]{:S(2)}, u32[]{:S(2)}) collective-permute-start(bf16[728,1152]{1,0:T(8,128)(2,1)} %add_convert_fusion.6), channel_id=1, source_target_pairs={{1,3},{5,7},{9,11},{13,15},{17,19},{21,23},{25,27},{29,31}} | collective-permute-start | bytes 5031944 | tf_op jit(solution)/shard_map/ppermute | solution.py:436
  832.1 35.8 %collective-permute-start.29 = (bf16[408,1152]{1,0:T(8,128)(2,1)}, bf16[408,1152]{1,0:T(8,128)(2,1)}, u32[]{:S(2)}, u32[]{:S(2)}) collective-permute-start(bf16[408,1152]{1,0:T(8,128)(2,1)} %reduce-scatter.22.cloned.1.call-done), channel_id=1, source_target_pairs={{3,2},{1,0},{7,6},{5,4},{11,10},{9,8},{15,14},{13,12},{19,18},{17,... | collective-permute-start | bytes 2820104 | tf_op jit(solution)/shard_map/ppermute | solution.py:436
  833.4 39.4 %collective-permute-start.24 = (bf16[728,1152]{1,0:T(8,128)(2,1)}, bf16[728,1152]{1,0:T(8,128)(2,1)S(1)}, u32[]{:S(2)}, u32[]{:S(2)}) collective-permute-start(bf16[728,1152]{1,0:T(8,128)(2,1)} %add_convert_fusion.5), channel_id=1, source_target_pairs={{1,2},{5,6},{9,10},{13,14},{17,18},{21,22},{25,26},{29,30}} | collective-permute-start | bytes 5031944 | tf_op jit(solution)/shard_map/ppermute | solution.py:436
  869.4 58.5 %collective-permute-start.30 = (bf16[408,1152]{1,0:T(8,128)(2,1)S(1)}, bf16[408,1152]{1,0:T(8,128)(2,1)S(1)}, u32[]{:S(2)}, u32[]{:S(2)}) collective-permute-start(bf16[408,1152]{1,0:T(8,128)(2,1)S(1)} %add_convert_fusion.9), channel_id=1, source_target_pairs={{2,0},{6,4},{10,8},{14,12},{18,16},{22,20},{26,24},{30,28}} | collective-permute-start | bytes 2820104 | tf_op jit(solution)/shard_map/ppermute | solution.py:436
  929.5 108.0 %all-gather.12.cloned.1.call-start = ((), (), s32[]{:S(2)}) async-start(), calls=%async_computation.9 | async-start | bytes 6635520 | tf_op jit(solution)/shard_map/all_gather | solution.py:571
  (127 other events, 2211.3 us)
Sparse Core Ops, SparseCore 0:
  51.8 74.9 all-gather.5
  147.7 106.9 all-gather.7
  274.3 83.0 all-gather.9
  507.7 74.1 reduce-scatter.15
  584.7 74.1 reduce-scatter.17
  662.3 74.1 reduce-scatter.19
  739.5 49.3 reduce-scatter.21
  827.9 57.4 reduce-scatter.13
  929.6 47.9 all-gather.13
  979.4 44.1 all-gather.11
where the time goes:
time: 1090 us; the launch traced here: 1080 us
  matrix products  328 us (30%)
  waiting for transfers between devices  292 us (27%)
  other arithmetic  153 us (14%)
  starting transfers between devices  108 us (10%)
  local copies, waits for them, and re-layouts  105 us (10%)
  Pallas kernels  74.5 us (7%)
  between operations  16.5 us (2%)
    ppermute x10, waiting for transfers between devices, advance(): moved = lax.ppermute(held, 'shard', pairs)  140 us
    dot_general x8, matrix products, contract_rows(): lax.dot_general(left_side, right_side, (((0,), (0,)), ((), ())), preferre...  100 us
    dot_general x4, matrix products, times_transposed(): lax.dot_general(left_side, right_side, (((1,), (1,)), ((), ())), preferre...  87 us
    pallas_call x2, Pallas kernels, adam_rows(): pl.pallas_call(body, grid_spec=pltpu.PrefetchScalarGridSpec(num_scalar_pr...  74.5 us
    ppermute x5, waiting for transfers between devices, moved(): return lax.ppermute(values, 'shard', pairs)  68 us
    ppermute x1, starting transfers between devices, spread_first(): near = lax.ppermute(rows, 'shard', [(0, 1), (2, 3)])  38.7 us
    dot_general x2, matrix products, input_grad_of(): jnp.dot(gate_low[first:last], w_gate_up[:hidden_width], preferred_element...  33.4 us
    convert_element_type x1, other arithmetic, per_device(): active.astype(jnp.bfloat16)  32.1 us
  transfers between devices with their start and end apart: 46, of which 19 were waited for; matrix products, arithmetic and copies ran while one was open for 40% of the time, Pallas kernels for 4%

commit v1 on v0

--- a/solution.py
+++ b/solution.py
@@ -403,7 +403,7 @@
         "down": (down_first, total_rows // split, product_rows(hidden_low, branch_low))
     }
     steps = {}
-    late_rows = early_rows // split
+    late_rows = qkv_rows // split
     segment_rows = owner_rows // split
 
     def bounds(key):
@@ -475,8 +475,16 @@
     attended_low = attended_grad.astype(jnp.bfloat16)
     out_rows = product_rows(mixed_low, attended_low)
 
-    factors["out"] = (qkv_rows // split, gate_first, out_rows)
-
+    def summed_out_rows(first, last):
+        rows = out_rows(first * 2, last * 2)
+        other = to_partner(one_parity(rows, 1 - core_index))
+        return add_low(one_parity(rows, core_index), other)
+
+    factors["out"] = (
+        qkv_rows // split,
+        gate_first,
+        summed_out_rows if tree else out_rows,
+    )
     mixed_grad = (
         times_transposed(attended_low, w_out)
         .astype(jnp.bfloat16)
@@ -540,17 +548,16 @@
     state = (params, first_moment, second_moment)
     if tree:
         qkv_grad = product_rows(qkv_low, normed_low)(0, qkv_rows)
-        late_grad = jnp.concatenate([qkv_grad, out_rows(0, query_width)], axis=0)
         by_piece = (
-            late_grad.reshape(wide_count // 2, -1, 2, 8, D)
+            qkv_grad.reshape(wide_count // 2, -1, 2, 8, D)
             .transpose(0, 2, 1, 3, 4)
-            .reshape(early_rows, D)
+            .reshape(qkv_rows, D)
         )
         steps[-1] = [lax.psum_scatter(by_piece, WIDE, scatter_dimension=0, tiled=True)]
         for key in (3, 2, 1, 0, -1):
             while len(steps[key]) < 3:
                 advance(key)
-        late_part = early_rows // wide_count
+        late_part = qkv_rows // wide_count
         early_part = owner_rows // wide_count - late_part
         whole_pieces = [steps[owner][-1] for owner in range(1, shard_count)]
         early_piece = choose_owner([steps[0][-1]] + [p[:early_part] for p in whole_pieces])
@@ -559,7 +566,7 @@
         early_groups, late_groups = early_part // 8, late_part // 8
         early_place = jnp.where(
             first_owner,
-            jnp.array([early_rows // 16, early_groups], jnp.int32),
+            jnp.array([qkv_rows // 16, early_groups], jnp.int32),
             jnp.array([0, early_groups + late_groups], jnp.int32),
         )
         late_place = jnp.where(

time: 1090 us -> 1060 us (0.972)
  waiting for transfers between devices: 292 us -> 264 us
    ppermute x10, waiting for transfers between devices: 140 us -> 107 us  [advance(): moved = lax.ppermute(held, 'shard', pairs)]
  transfers between devices with their start and end apart: 46 -> 47, of which waited for: 19 -> 20; matrix products, arithmetic and copies ran while one was open for 40% -> 42% of each run, Pallas kernels for 4% -> 5%
where the time goes in v1:
time: 1060 us; the launch traced here: 1050 us
  matrix products  324 us (31%)
  waiting for transfers between devices  264 us (25%)
  other arithmetic  159 us (15%)
  starting transfers between devices  107 us (10%)
  local copies, waits for them, and re-layouts  103 us (10%)
  Pallas kernels  74.1 us (7%)
  between operations  16.5 us (2%)
    ppermute x10, waiting for transfers between devices, advance(): moved = lax.ppermute(held, 'shard', pairs)  107 us
    dot_general x8, matrix products, contract_rows(): lax.dot_general(left_side, right_side, (((0,), (0,)), ((), ())), preferre...  97.3 us
    dot_general x4, matrix products, times_transposed(): lax.dot_general(left_side, right_side, (((1,), (1,)), ((), ())), preferre...  87.3 us
    pallas_call x2, Pallas kernels, adam_rows(): pl.pallas_call(body, grid_spec=pltpu.PrefetchScalarGridSpec(num_scalar_pr...  74.1 us
    ppermute x5, waiting for transfers between devices, moved(): return lax.ppermute(values, 'shard', pairs)  68.1 us
    ppermute x1, starting transfers between devices, spread_first(): near = lax.ppermute(rows, 'shard', [(0, 1), (2, 3)])  38.7 us
    dot_general x2, matrix products, input_grad_of(): jnp.dot(gate_low[first:last], w_gate_up[:hidden_width], preferred_element...  32.5 us
    convert_element_type x1, other arithmetic, per_device(): active.astype(jnp.bfloat16)  32.1 us
  transfers between devices with their start and end apart: 47, of which 20 were waited for; matrix products, arithmetic and copies ran while one was open for 42% of the time, Pallas kernels for 5%

profile of v1, /device:TPU:0, one launch (start us, length us, event | category | flops | bytes accessed | tf_op | source)
XLA Modules:
  0.0 1048.7 jit_solution(10179908790903742123)
XLA Ops:
  14.9 36.7 %collective-permute-done.13 = bf16[728,1152]{1,0:T(8,128)(2,1)} collective-permute-done((bf16[728,1152]{1,0:T(8,128)(2,1)S(1)}, bf16[728,1152]{1,0:T(8,128)(2,1)}, u32[]{:S(2)}, u32[]{:S(2)}) %collective-permute-start.13) | collective-permute-done | bytes 1677344 | tf_op jit(solution)/shard_map/ppermute | solution.py:211
  62.4 12.5 %collective-permute-done.3 = bf16[320,1152]{1,0:T(8,128)(2,1)} collective-permute-done((bf16[320,1152]{1,0:T(8,128)(2,1)S(1)}, bf16[320,1152]{1,0:T(8,128)(2,1)}, u32[]{:S(2)}, u32[]{:S(2)}) %collective-permute-start.3) | collective-permute-done | bytes 737312 | tf_op jit(solution)/shard_map/ppermute | solution.py:136
  76.4 38.7 %collective-permute-start.4 = (bf16[320,1152]{1,0:T(8,128)(2,1)S(1)}, bf16[320,1152]{1,0:T(8,128)(2,1)}, u32[]{:S(2)}, u32[]{:S(2)}) collective-permute-start(bf16[320,1152]{1,0:T(8,128)(2,1)S(1)} %broadcast_select_fusion.2), channel_id=1, source_target_pairs={{0,1},{2,3},{4,5},{6,7},{8,9},{10,11},{12,13},{14,15},{16,17},{18,... | collective-permute-start | bytes 2211848 | tf_op jit(solution)/shard_map/ppermute | solution.py:138
  118.2 10.1 collective-permute-done.4
  131.1 13.6 %collective-permute-done.15 = bf16[728,1152]{1,0:T(8,128)(2,1)} collective-permute-done((bf16[728,1152]{1,0:T(8,128)(2,1)}, bf16[728,1152]{1,0:T(8,128)(2,1)}, u32[]{:S(2)}, u32[]{:S(2)}) %collective-permute-start.15) | collective-permute-done | bytes 1677344 | tf_op jit(solution)/shard_map/ppermute | solution.py:211
  147.6 9.1 broadcast_in_dim.104
  176.5 20.2 %collective-permute-done.6 = bf16[320,1152]{1,0:T(8,128)(2,1)} collective-permute-done((bf16[320,1152]{1,0:T(8,128)(2,1)}, bf16[320,1152]{1,0:T(8,128)(2,1)}, u32[]{:S(2)}, u32[]{:S(2)}) %collective-permute-start.6) | collective-permute-done | bytes 737312 | tf_op jit(solution)/shard_map/ppermute | solution.py:146
  199.0 19.2 %collective-permute-start.2 = (bf16[4,288]{1,0:T(4,128)(2,1)S(1)}, bf16[4,288]{1,0:T(4,128)(2,1)S(1)}, u32[]{:S(2)}, u32[]{:S(2)}) collective-permute-start(bf16[4,288]{1,0:T(4,128)(2,1)S(1)} %convert_element_type.254), channel_id=1, source_target_pairs={{0,3},{1,0},{2,1},{3,2},{4,7},{5,4},{6,5},{7,6},{8,11},{9,8},{10,9... | collective-permute-start | bytes 6920 | tf_op jit(solution)/shard_map/ppermute | solution.py:128
  253.7 17.7 %collective-permute-done.17 = bf16[728,1152]{1,0:T(8,128)(2,1)} collective-permute-done((bf16[728,1152]{1,0:T(8,128)(2,1)}, bf16[728,1152]{1,0:T(8,128)(2,1)}, u32[]{:S(2)}, u32[]{:S(2)}) %collective-permute-start.17) | collective-permute-done | bytes 1677344 | tf_op jit(solution)/shard_map/ppermute | solution.py:211
  274.5 27.0 %while.31 = (s32[]{:T(128)}, bf16[2,512,1,4,256]{4,1,3,2,0:T(8,128)(2,1)}, f32[2,1,4,512,1]{3,2,4,1,0:T(4,128)S(1)}, s32[2,512]{1,0:T(2,128)S(1)}, s32[1024]{0:T...) while((s32[]{:T(128)}, ...), condition=%wide.region_6.7_spmd.clone, body=%wide.region_3.6_spmd.sunk.clone | while | flops 2186279424 | bytes 50411736 | solution.py:355
  330.3 27.1 %all-gather.10.cloned.1.call-done = bf16[2912,1152]{1,0:T(8,128)(2,1)} async-done(((bf16[728,1152]{1,0:T(8,128)(2,1)}), bf16[2912,1152]{1,0:T(8,128)(2,1)}) %all-gather.10.cloned.1.call-update) | async-done | bytes 6709264 | tf_op jit(solution)/shard_map/all_gather | solution.py:229
  363.7 45.1 %convolution_convert_fusion = bf16[2048,6912]{1,0:T(8,128)(2,1)} fusion(bf16[11648,1152]{1,0:T(8,128)(2,1)} %constant_dynamic-update-slice_fusion.1, bf16[1024,1152]{1,0:T(8,128)(2,1)} %collective-permute-done.12, bf16[1024,1152]{1,0:T(8,128)(2,1)S(1)} %multiply_convert_fusion.2), kind=kOutput, calls=%fused_computation.94 | convolution fusion | flops 32638500864 | bytes 48955392 | tf_op jit(solution)/shard_map/dot_general | solution.py:74
  408.9 32.1 %fusion.75 = (bf16[2048,3456]{1,0:T(8,128)(2,1)}, bf16[2048,3456]{1,0:T(8,128)(2,1)}, bf16[2048,3456]{1,0:T(8,128)(2,1)}) fusion(bf16[2048,6912]{1,0:T(8,128)(2,1)} %convolution_convert_fusion), kind=kLoop, calls=%fused_computation.95 | loop fusion | flops 176947200 | bytes 70778880 | tf_op jit(solution)/shard_map/convert_element_type | solution.py:374
  441.0 15.8 %fusion.98 = f32[1024,1152]{1,0:T(8,128)} fusion(bf16[2048,3456]{1,0:T(8,128)(2,1)} %get-tuple-element.243, bf16[11648,1152]{1,0:T(8,128)(2,1)} %constant_dynamic-update-slice_fusion.1), kind=kOutput, calls=%fused_computation.124 | convolution fusion | flops 8153726976 | bytes 19759104 | tf_op jit(solution)/shard_map/dot_general | solution.py:377
  456.8 14.5 %fusion.96 = f32[1024,1152]{1,0:T(8,128)} fusion(bf16[2048,3456]{1,0:T(8,128)(2,1)S(1)} %copy-done.13, bf16[11648,1152]{1,0:T(8,128)(2,1)} %constant_dynamic-update-slice_fusion.1), kind=kOutput, calls=%fused_computation.122 | convolution fusion | flops 8153726976 | bytes 19759104 | tf_op jit(solution)/shard_map/dot_general | solution.py:382
  485.2 22.4 %fusion.79 = bf16[2912,1152]{1,0:T(8,128)(2,1)} fusion(bf16[2048,3456]{1,0:T(8,128)(2,1)} %get-tuple-element.243, bf16[1024,1152]{1,0:T(8,128)(2,1)S(1)} %collective-permute-done.19, bf16[1024,1152]{1,0:T(8,128)(2,1)S(1)} %get-tuple-element.470), kind=kOutput, calls=%fused_computation.100 | convolution fusion | flops 13753331712 | bytes 23486464 | tf_op jit(solution)/shard_map/dot_general | solution.py:68
  517.9 32.1 %multiply_convert_fusion = (bf16[2048,3456]{1,0:T(8,128)(2,1)}, bf16[2048,3456]{1,0:T(8,128)(2,1)}) fusion(bf16[2048,3456]{1,0:T(8,128)(2,1)} %get-tuple-element.249, bf16[2048,3456]{1,0:T(8,128)(2,1)} %get-tuple-element.248, bf16[2048,1152]{1,0:T(8,128)(2,1)} %pad_maximum_fusion.4, bf16[11648,1152]{1,0:T(8,128)(2,1)} %constant_dynamic-update-slice_fusion.1), kind=kOutput, calls=%fused_computation.92 | convolution fusion | flops 16349921280 | bytes 69304320 | tf_op jit(solution)/shard_map/dot_general | solution.py:74
  550.0 20.1 %convolution_convert_fusion.1 = bf16[2368,1152]{1,0:T(8,128)(2,1)} fusion(bf16[2048,3456]{1,0:T(8,128)(2,1)} %get-tuple-element.255, bf16[1024,1152]{1,0:T(8,128)(2,1)} %collective-permute-done.12, bf16[1024,1152]{1,0:T(8,128)(2,1)S(1)} %copy-done.28), kind=kOutput, calls=%fused_computation.101 | convolution fusion | flops 11185790976 | bytes 20135936 | tf_op jit(solution)/shard_map/dot_general | solution.py:68
  576.2 9.9 convolution_convert_fusion.4
  586.1 14.5 %fusion.85 = bf16[1824,1152]{1,0:T(8,128)(2,1)S(1)} fusion(bf16[2048,3456]{1,0:T(8,128)(2,1)} %get-tuple-element.254, bf16[1024,1152]{1,0:T(8,128)(2,1)} %collective-permute-done.12, bf16[1024,1152]{1,0:T(8,128)(2,1)S(1)} %copy-done.29), kind=kOutput, calls=%fused_computation.111 | convolution fusion | flops 8618250240 | bytes 16785408 | tf_op jit(solution)/shard_map/dot_general | solution.py:68
  604.0 13.2 %fusion.92 = f32[1024,1152]{1,0:T(8,128)S(1)} fusion(bf16[2048,3456]{1,0:T(8,128)(2,1)} %get-tuple-element.255, bf16[11648,1152]{1,0:T(8,128)(2,1)} %constant_dynamic-update-slice_fusion.1), kind=kOutput, calls=%fused_computation.118 | convolution fusion | flops 8153726976 | bytes 19759104 | tf_op jit(solution)/shard_map/dot_general | solution.py:461
  617.3 15.8 %fusion.115 = f32[1024,1152]{1,0:T(8,128)} fusion(f32[1024,1152]{1,0:T(8,128)S(1)} %fusion.92, bf16[11648,1152]{1,0:T(8,128)(2,1)} %constant_dynamic-update-slice_fusion.1, bf16[2048,3456]{1,0:T(8,128)(2,1)} %get-tuple-element.254), kind=kOutput, calls=%fused_computation.151 | convolution fusion | flops 8154906624 | bytes 24477696 | tf_op jit(solution)/shard_map/dot_general | solution.py:459
  635.7 15.3 %convolution_convert_fusion.3 = bf16[1632,1152]{1,0:T(8,128)(2,1)} fusion(bf16[2048,3456]{1,0:T(8,128)(2,1)} %get-tuple-element.254, bf16[1024,1152]{1,0:T(8,128)(2,1)} %collective-permute-done.12, bf16[1024,1152]{1,0:T(8,128)(2,1)S(1)} %copy-done.30), kind=kOutput, calls=%fused_computation.112 | convolution fusion | flops 7712059392 | bytes 15294464 | tf_op jit(solution)/shard_map/dot_general | solution.py:68
  655.8 13.3 %fusion.88 = f32[1024,1152]{1,0:T(8,128)S(1)} fusion(bf16[2048,3456]{1,0:T(8,128)(2,1)} %get-tuple-element.255, bf16[11648,1152]{1,0:T(8,128)(2,1)} %constant_dynamic-update-slice_fusion.1), kind=kOutput, calls=%fused_computation.114 | convolution fusion | flops 8153726976 | bytes 19759104 | tf_op jit(solution)/shard_map/dot_general | solution.py:461
  669.1 16.6 %fusion.125 = f32[1024,1152]{1,0:T(8,128)} fusion(f32[1024,1152]{1,0:T(8,128)} %collective-permute-done.20, f32[1024,1152]{1,0:T(8,128)S(1)} %fusion.88, bf16[11648,1152]{1,0:T(8,128)(2,1)} %constant_dynamic-update-slice_fusion.1, bf16[2048,3456]{1,0:T(8,128)(2,1)} %get-tuple-element.254), kind=kOutput, calls=%fused_computation.153 | convolution fusion | flops 8156086272 | bytes 29196288 | tf_op jit(solution)/shard_map/dot_general | solution.py:459
  730.5 48.7 %while.32 = (s32[]{:T(128)}, f32[1024,1,256]{0,2,1:T(8,128)S(1)}, f32[1024,1,256]{0,2,1:T(8,128)}, f32[2,512,1,4,256]{4,1,3,2,0:T(8,128)}, bf16[2,512,1,4,256]{4...) while((s32[]{:T(128)}, f32[1024,1,256]{0,2,1:T(8,128)S(1)}, ...), condition=%wide.region_17.18_spmd.clone.clone, body=%wide.region_15.17_spmd.clone.sunk.clone | while | flops 5423233536 | bytes 125376864 | solution.py:526
  813.0 21.6 %collective-permute-done.26 = bf16[728,1152]{1,0:T(8,128)(2,1)} collective-permute-done((bf16[728,1152]{1,0:T(8,128)(2,1)}, bf16[728,1152]{1,0:T(8,128)(2,1)}, u32[]{:S(2)}, u32[]{:S(2)}) %collective-permute-start.26) | collective-permute-done | bytes 1677344 | tf_op jit(solution)/shard_map/ppermute | solution.py:436
  851.6 55.5 %collective-permute-done.31 = bf16[536,1152]{1,0:T(8,128)(2,1)S(1)} collective-permute-done((bf16[536,1152]{1,0:T(8,128)(2,1)S(1)}, bf16[536,1152]{1,0:T(8,128)(2,1)S(1)}, u32[]{:S(2)}, u32[]{:S(2)}) %collective-permute-start.31) | collective-permute-done | bytes 1234976 | tf_op jit(solution)/shard_map/ppermute | solution.py:436
  910.3 11.4 %collective-permute-done.28 = bf16[192,1152]{1,0:T(8,128)(2,1)S(1)} collective-permute-done((bf16[192,1152]{1,0:T(8,128)(2,1)}, bf16[192,1152]{1,0:T(8,128)(2,1)S(1)}, u32[]{:S(2)}, u32[]{:S(2)}) %collective-permute-start.28) | collective-permute-done | bytes 442400 | tf_op jit(solution)/shard_map/ppermute | solution.py:436
  924.3 11.1 %collective-permute-done.29 = bf16[192,1152]{1,0:T(8,128)(2,1)S(1)} collective-permute-done((bf16[192,1152]{1,0:T(8,128)(2,1)S(1)}, bf16[192,1152]{1,0:T(8,128)(2,1)S(1)}, u32[]{:S(2)}, u32[]{:S(2)}) %collective-permute-start.29) | collective-permute-done | bytes 442400 | tf_op jit(solution)/shard_map/ppermute | solution.py:436
  967.6 52.0 %adam_rows.2 = (f32[364,2,8,1152]{3,2,1,0:T(8,128)}, f32[364,2,8,1152]{3,2,1,0:T(8,128)}, f32[364,2,8,1152]{3,2,1,0:T(8,128)}, f32[364,2,8,1152]{3,2,1,0:T(8,128)}) custom-call(s32[2]{0:T(128)} %broadcast_select_fusion.14.place_ref, bf16[4288,1152]{1,0:T(8,128)(2,1)} %all-gather.14.cloned.1.call-done.grad_ref, f32[364,2,8,1152]{3,2,1,0:T(8,128)} %bitcast.323, ...), custom_call_target="tpu_custom_call" | custom-call | flops 98795520 | bytes 148193280 | tf_op jit(solution)/shard_map/adam_rows/pallas_call | solution.py:253
  1019.6 22.1 %adam_rows.3 = (f32[364,2,8,1152]{3,2,1,0:T(8,128)}, f32[364,2,8,1152]{3,2,1,0:T(8,128)}, f32[364,2,8,1152]{3,2,1,0:T(8,128)}, f32[364,2,8,1152]{3,2,1,0:T(8,128)}) custom-call(s32[2]{0:T(128)} %broadcast_select_fusion.15.place_ref, ...), custom_call_target="tpu_custom_call", output_to_operand_aliasing={{0}: (5, {}), {1}: (6, {}), {2}: (7, {}), {3}: (8, {})} | custom-call | flops 35389440 | bytes 53084160 | tf_op jit(solution)/shard_map/adam_rows/pallas_call | solution.py:253
  (478 shorter events, 372.0 us)
Async XLA Ops:
  7.2 309.2 %all-gather.6.cloned.1.call-start = ((), (), s32[]{:S(2)}) async-start(), calls=%async_computation.5 | async-start | bytes 8386560 | tf_op jit(solution)/shard_map/all_gather | solution.py:229
  11.8 39.8 %collective-permute-start.13 = (bf16[728,1152]{1,0:T(8,128)(2,1)S(1)}, bf16[728,1152]{1,0:T(8,128)(2,1)}, u32[]{:S(2)}, u32[]{:S(2)}) collective-permute-start(bf16[728,1152]{1,0:T(8,128)(2,1)S(1)} %fusion.148), channel_id=1, source_target_pairs={{0,1},{1,0},{2,3},{3,2},{4,5},{5,4},{6,7},{7,6},{8,9},{9,8},{10,11... | collective-permute-start | bytes 5031944 | tf_op jit(solution)/shard_map/ppermute | solution.py:211
  51.7 272.4 %all-gather.8.cloned.1.call-start = ((), (), s32[]{:S(2)}) async-start(), calls=%async_computation.6 | async-start | bytes 8386560 | tf_op jit(solution)/shard_map/all_gather | solution.py:229
  61.1 83.6 %collective-permute-start.15 = (bf16[728,1152]{1,0:T(8,128)(2,1)}, bf16[728,1152]{1,0:T(8,128)(2,1)}, u32[]{:S(2)}, u32[]{:S(2)}) collective-permute-start(bf16[728,1152]{1,0:T(8,128)(2,1)} %collective-permute-done.14), channel_id=1, source_target_pairs={{1,0},{2,3},{5,4},{6,7},{9,8},{10,11},{13,12},{14,15},{17,16},{18,... | collective-permute-start | bytes 5031944 | tf_op jit(solution)/shard_map/ppermute | solution.py:211
  76.4 51.9 %collective-permute-start.4 = (bf16[320,1152]{1,0:T(8,128)(2,1)S(1)}, bf16[320,1152]{1,0:T(8,128)(2,1)}, u32[]{:S(2)}, u32[]{:S(2)}) collective-permute-start(bf16[320,1152]{1,0:T(8,128)(2,1)S(1)} %broadcast_select_fusion.2), channel_id=1, source_target_pairs={{0,1},{2,3},{4,5},{6,7},{8,9},{10,11},{12,13},{14,15},{16,17},{18,... | collective-permute-start | bytes 2211848 | tf_op jit(solution)/shard_map/ppermute | solution.py:138
  115.1 103.5 %collective-permute-start.1 = (bf16[4,288]{1,0:T(4,128)(2,1)S(1)}, bf16[4,288]{1,0:T(4,128)(2,1)S(1)}, u32[]{:S(2)}, u32[]{:S(2)}) collective-permute-start(bf16[4,288]{1,0:T(4,128)(2,1)S(1)} %convert_element_type.254), channel_id=1, source_target_pairs={{0,2},{1,3},{2,0},{3,1},{4,6},{5,7},{6,4},{7,5},{8,10},{9,11},{10,... | collective-permute-start | bytes 6920 | tf_op jit(solution)/shard_map/ppermute | solution.py:128
  116.4 82.6 %collective-permute-start = (bf16[4,288]{1,0:T(4,128)(2,1)S(1)}, bf16[4,288]{1,0:T(4,128)(2,1)S(1)}, u32[]{:S(2)}, u32[]{:S(2)}) collective-permute-start(bf16[4,288]{1,0:T(4,128)(2,1)S(1)} %convert_element_type.254), channel_id=1, source_target_pairs={{0,1},{1,2},{2,3},{3,0},{4,5},{5,6},{6,7},{7,4},{8,9},{9,10},{10,1... | collective-permute-start | bytes 6920 | tf_op jit(solution)/shard_map/ppermute | solution.py:128
  129.5 35.5 %collective-permute-start.5 = (bf16[320,1152]{1,0:T(8,128)(2,1)S(1)}, bf16[320,1152]{1,0:T(8,128)(2,1)}, u32[]{:S(2)}, u32[]{:S(2)}) collective-permute-start(bf16[320,1152]{1,0:T(8,128)(2,1)S(1)} %broadcast_select_fusion.3), channel_id=1, source_target_pairs={{0,16},{4,20},{8,24},{12,28},{16,0},{20,4},{24,8},{28,12},{1,17},{... | collective-permute-start | bytes 2211848 | tf_op jit(solution)/shard_map/ppermute | solution.py:146
  147.5 209.9 %all-gather.10.cloned.1.call-start = ((), (), s32[]{:S(2)}) async-start(), calls=%async_computation.7 | async-start | bytes 8386560 | tf_op jit(solution)/shard_map/all_gather | solution.py:229
  167.4 29.3 %collective-permute-start.6 = (bf16[320,1152]{1,0:T(8,128)(2,1)}, bf16[320,1152]{1,0:T(8,128)(2,1)}, u32[]{:S(2)}, u32[]{:S(2)}) collective-permute-start(bf16[320,1152]{1,0:T(8,128)(2,1)} %get-tuple-element.480), channel_id=1, source_target_pairs={{0,8},{4,12},{8,0},{12,4},{16,24},{20,28},{24,16},{28,20},{1,9},{5... | collective-permute-start | bytes 2211848 | tf_op jit(solution)/shard_map/ppermute | solution.py:146
  170.9 52.3 %collective-permute-start.16 = (bf16[728,1152]{1,0:T(8,128)(2,1)}, bf16[728,1152]{1,0:T(8,128)(2,1)}, u32[]{:S(2)}, u32[]{:S(2)}) collective-permute-start(bf16[728,1152]{1,0:T(8,128)(2,1)} %collective-permute-done.13), channel_id=1, source_target_pairs={{1,2},{2,1},{5,6},{6,5},{9,10},{10,9},{13,14},{14,13},{17,18},{18,... | collective-permute-start | bytes 5031944 | tf_op jit(solution)/shard_map/ppermute | solution.py:211
  175.9 44.4 %collective-permute-start.9 = (bf16[320,1152]{1,0:T(8,128)(2,1)}, bf16[320,1152]{1,0:T(8,128)(2,1)}, u32[]{:S(2)}, u32[]{:S(2)}) collective-permute-start(bf16[320,1152]{1,0:T(8,128)(2,1)} %get-tuple-element.479), channel_id=1, source_target_pairs={{0,8},{4,12},{8,0},{12,4},{16,24},{20,28},{24,16},{28,20},{1,9},{5... | collective-permute-start | bytes 2211848 | tf_op jit(solution)/shard_map/ppermute | solution.py:146
  199.0 25.7 %collective-permute-start.7 = (bf16[320,1152]{1,0:T(8,128)(2,1)}, bf16[320,1152]{1,0:T(8,128)(2,1)}, u32[]{:S(2)}, u32[]{:S(2)}) collective-permute-start(bf16[320,1152]{1,0:T(8,128)(2,1)} %get-tuple-element.482), channel_id=1, source_target_pairs={{0,4},{4,0},{8,12},{12,8},{16,20},{20,16},{24,28},{28,24},{1,5},{5... | collective-permute-start | bytes 2211848 | tf_op jit(solution)/shard_map/ppermute | solution.py:146
  199.0 20.5 %collective-permute-start.2 = (bf16[4,288]{1,0:T(4,128)(2,1)S(1)}, bf16[4,288]{1,0:T(4,128)(2,1)S(1)}, u32[]{:S(2)}, u32[]{:S(2)}) collective-permute-start(bf16[4,288]{1,0:T(4,128)(2,1)S(1)} %convert_element_type.254), channel_id=1, source_target_pairs={{0,3},{1,0},{2,1},{3,2},{4,7},{5,4},{6,5},{7,6},{8,11},{9,8},{10,9... | collective-permute-start | bytes 6920 | tf_op jit(solution)/shard_map/ppermute | solution.py:128
  222.7 83.5 %collective-permute-start.11 = (bf16[320,1152]{1,0:T(8,128)(2,1)}, bf16[320,1152]{1,0:T(8,128)(2,1)}, u32[]{:S(2)}, u32[]{:S(2)}) collective-permute-start(bf16[320,1152]{1,0:T(8,128)(2,1)} %get-tuple-element.477), channel_id=1, source_target_pairs={{0,4},{4,0},{8,12},{12,8},{16,20},{20,16},{24,28},{28,24},{1,5},{5... | collective-permute-start | bytes 2211848 | tf_op jit(solution)/shard_map/ppermute | solution.py:146
  223.2 48.2 %collective-permute-start.17 = (bf16[728,1152]{1,0:T(8,128)(2,1)}, bf16[728,1152]{1,0:T(8,128)(2,1)}, u32[]{:S(2)}, u32[]{:S(2)}) collective-permute-start(bf16[728,1152]{1,0:T(8,128)(2,1)} %collective-permute-done.16), channel_id=1, source_target_pairs={{1,0},{2,3},{5,4},{6,7},{9,8},{10,11},{13,12},{14,15},{17,16},{18,... | collective-permute-start | bytes 5031944 | tf_op jit(solution)/shard_map/ppermute | solution.py:211
  274.2 329.8 %reduce-scatter.16.cloned.1.call-start = ((), (), s32[]{:S(2)}) async-start(), calls=%async_computation.11 | async-start | bytes 8386560
  316.3 47.4 %collective-permute-start.12 = (bf16[1024,1152]{1,0:T(8,128)(2,1)S(1)}, bf16[1024,1152]{1,0:T(8,128)(2,1)}, u32[]{:S(2)}, u32[]{:S(2)}) collective-permute-start(bf16[1024,1152]{1,0:T(8,128)(2,1)S(1)} %multiply_convert_fusion.2), channel_id=1, source_target_pairs={{0,4},{4,0},{1,5},{5,1},{2,6},{6,2},{3,7},{7,3},{8,12},{12,8},{9,1... | collective-permute-start | bytes 7077896 | tf_op jit(solution)/shard_map/ppermute | solution.py:178
  507.6 178.2 %reduce-scatter.18.cloned.1.call-start = ((), (), s32[]{:S(2)}) async-start(), calls=%async_computation.12 | async-start | bytes 8386560
  576.0 211.5 %reduce-scatter.20.cloned.1.call-start = ((), (), s32[]{:S(2)}) async-start(), calls=%async_computation.13 | async-start | bytes 8386560
  633.1 36.0 %collective-permute-start.20 = (f32[1024,1152]{1,0:T(8,128)}, f32[1024,1152]{1,0:T(8,128)}, u32[]{:S(2)}, u32[]{:S(2)}) collective-permute-start(f32[1024,1152]{1,0:T(8,128)} %fusion.115), channel_id=1, source_target_pairs={{0,4},{4,0},{1,5},{5,1},{2,6},{6,2},{3,7},{7,3},{8,12},{12,8},{9,1... | collective-permute-start | bytes 14155784 | tf_op jit(solution)/shard_map/ppermute | solution.py:178
  635.6 175.8 %reduce-scatter.22.cloned.1.call-start = ((), (), s32[]{:S(2)}) async-start(), calls=%async_computation.14 | async-start | bytes 6174720
  651.0 55.2 %collective-permute-start.22 = (bf16[728,1152]{1,0:T(8,128)(2,1)}, bf16[728,1152]{1,0:T(8,128)(2,1)}, u32[]{:S(2)}, u32[]{:S(2)}) collective-permute-start(bf16[728,1152]{1,0:T(8,128)(2,1)} %reduce-scatter.16.cloned.1.call-done), channel_id=1, source_target_pairs={{0,1},{2,3},{4,5},{6,7},{8,9},{10,11},{12,13},{14,15},{16,17},{18,... | collective-permute-start | bytes 5031944 | tf_op jit(solution)/shard_map/ppermute | solution.py:436
  720.1 64.3 %collective-permute-start.23 = (bf16[728,1152]{1,0:T(8,128)(2,1)}, bf16[728,1152]{1,0:T(8,128)(2,1)}, u32[]{:S(2)}, u32[]{:S(2)}) collective-permute-start(bf16[728,1152]{1,0:T(8,128)(2,1)} %reduce-scatter.18.cloned.1.call-done), channel_id=1, source_target_pairs={{3,2},{0,1},{7,6},{4,5},{11,10},{8,9},{15,14},{12,13},{19,18},{16,... | collective-permute-start | bytes 5031944 | tf_op jit(solution)/shard_map/ppermute | solution.py:436
  728.9 180.1 %reduce-scatter.14.cloned.1.call-start = ((), (), s32[]{:S(2)}) async-start(), calls=%async_computation.8 | async-start | bytes 3981312 | tf_op jit(solution)/shard_map/reduce_scatter | solution.py:556
  796.4 38.2 %collective-permute-start.26 = (bf16[728,1152]{1,0:T(8,128)(2,1)}, bf16[728,1152]{1,0:T(8,128)(2,1)}, u32[]{:S(2)}, u32[]{:S(2)}) collective-permute-start(bf16[728,1152]{1,0:T(8,128)(2,1)} %reduce-scatter.20.cloned.1.call-done), channel_id=1, source_target_pairs={{0,1},{3,2},{4,5},{7,6},{8,9},{11,10},{12,13},{15,14},{16,17},{19,... | collective-permute-start | bytes 5031944 | tf_op jit(solution)/shard_map/ppermute | solution.py:436
  807.6 160.1 %all-gather.14.cloned.1.call-start = ((), (), s32[]{:S(2)}) async-start(), calls=%async_computation.10 | async-start | bytes 11114496 | tf_op jit(solution)/shard_map/all_gather | solution.py:577
  807.6 30.3 %collective-permute-start.24 = (bf16[728,1152]{1,0:T(8,128)(2,1)}, bf16[728,1152]{1,0:T(8,128)(2,1)}, u32[]{:S(2)}, u32[]{:S(2)}) collective-permute-start(bf16[728,1152]{1,0:T(8,128)(2,1)} %add_convert_fusion.6), channel_id=1, source_target_pairs={{1,3},{5,7},{9,11},{13,15},{17,19},{21,23},{25,27},{29,31}} | collective-permute-start | bytes 5031944 | tf_op jit(solution)/shard_map/ppermute | solution.py:436
  809.5 39.4 %collective-permute-start.25 = (bf16[728,1152]{1,0:T(8,128)(2,1)}, bf16[728,1152]{1,0:T(8,128)(2,1)}, u32[]{:S(2)}, u32[]{:S(2)}) collective-permute-start(bf16[728,1152]{1,0:T(8,128)(2,1)} %add_convert_fusion.5), channel_id=1, source_target_pairs={{1,2},{5,6},{9,10},{13,14},{17,18},{21,22},{25,26},{29,30}} | collective-permute-start | bytes 5031944 | tf_op jit(solution)/shard_map/ppermute | solution.py:436
  811.4 35.9 %collective-permute-start.30 = (bf16[536,1152]{1,0:T(8,128)(2,1)}, bf16[536,1152]{1,0:T(8,128)(2,1)S(1)}, u32[]{:S(2)}, u32[]{:S(2)}) collective-permute-start(bf16[536,1152]{1,0:T(8,128)(2,1)} %reduce-scatter.22.cloned.1.call-done), channel_id=1, source_target_pairs={{3,2},{1,0},{7,6},{5,4},{11,10},{9,8},{15,14},{13,12},{19,18},{17,... | collective-permute-start | bytes 3704840 | tf_op jit(solution)/shard_map/ppermute | solution.py:436
  847.6 59.5 %collective-permute-start.31 = (bf16[536,1152]{1,0:T(8,128)(2,1)S(1)}, bf16[536,1152]{1,0:T(8,128)(2,1)S(1)}, u32[]{:S(2)}, u32[]{:S(2)}) collective-permute-start(bf16[536,1152]{1,0:T(8,128)(2,1)S(1)} %add_convert_fusion.8), channel_id=1, source_target_pairs={{2,0},{6,4},{10,8},{14,12},{18,16},{22,20},{26,24},{30,28}} | collective-permute-start | bytes 3704840 | tf_op jit(solution)/shard_map/ppermute | solution.py:436
  909.0 110.7 %all-gather.12.cloned.1.call-start = ((), (), s32[]{:S(2)}) async-start(), calls=%async_computation.9 | async-start | bytes 3981312 | tf_op jit(solution)/shard_map/all_gather | solution.py:578
  (127 other events, 2303.2 us)
Sparse Core Ops, SparseCore 0:
  51.8 74.9 all-gather.5
  147.7 106.9 all-gather.7
  274.4 83.0 all-gather.9
  507.7 74.1 reduce-scatter.15
  584.7 74.1 reduce-scatter.17
  662.3 74.1 reduce-scatter.19
  740.1 59.2 reduce-scatter.21
  807.7 50.1 reduce-scatter.13
  909.1 58.4 all-gather.13
  969.4 33.4 all-gather.11
